TPU v7x, 256 devices: a whole 4x4x8 slice. The times are simulated.
256 devices in a mesh: band: 64 (over x, z, core), rep: 4 (over y).
Axes of the slice: x: 4, y: 4, z: 8, core: 2. Of those that a mesh axis runs over, the one named last changes fastest.
Arguments:
- patches: bfloat16 [8, 4, 80, 64, 768], P('rep', None, None, 'band'), may hold values from -6 to 6
- variable_group_index: int32 [5], replicated, may hold values from 0 to 2, as said below
- frozen_patch_weight: bfloat16 [3, 16, 512], replicated, may hold values from -0.625 to 0.625
- adapter_down: bfloat16 [80, 16], P('rep'), may hold values from -0.625 to 0.625
- adapter_up: bfloat16 [16, 512], P(None, 'rep'), may hold values from -1.5 to 1.5
- level_merge_weight: bfloat16 [4, 512, 512], replicated, may hold values from -0.125 to 0.125
- window_patch_mixer: bfloat16 [96, 96], replicated, may hold values from -0.625 to 0.625
- column_block_owner: int32 [64], replicated, may hold values from 0 to 63, each once
- mixed_token_gradient: bfloat16 [8, 64, 64, 12, 512], P('rep', 'band'), may hold values from -0.01171875 to 0.01171875
Outputs:
- mixed: bfloat16 [8, 64, 64, 12, 512], P('rep', 'band')
- first_factor_gradient: float32 [80, 16], P('rep')
- second_factor_gradient: float32 [16, 512], P(None, 'rep')
Inputs may be any that keep to these rules, and one draw needn't show every extreme that they name: Column block j goes to the band device column_block_owner[j]; each device owns one block. `variable_group_index`: every one of the 3 groups holds at least one variable.
All inputs are finite; a program needn't handle non-finite values.
Results may differ from a plain program's by a relative error of at most 0.01.
Values may be sent and summed in bfloat16 or wider, within the bound.
A program may use at most 128 MiB of HBM per device.

v0:
```python
import jax
import jax.numpy as jnp
from jax import lax
from jax.sharding import PartitionSpec as P

WLAT = 8
WLON = 12


def gelu_exact(values):
    return jax.nn.gelu(values, approximate=False)


def embed_tokens(pixels, merged, level_merge_weight):
    embedded = jnp.einsum(
        "nlkt,kd->nltd", pixels, merged, preferred_element_type=jnp.float32
    ).astype(jnp.bfloat16)
    return jnp.einsum(
        "nltd,lde->nte", embedded, level_merge_weight, preferred_element_type=jnp.float32
    ).astype(jnp.bfloat16)


def window_forward(tokens, mix_table):
    item_count, lat_rows, block_width, feature_dim = tokens.shape
    window_tiles = tokens.reshape(
        item_count, lat_rows // WLAT, WLAT, block_width // WLON, WLON, feature_dim
    )
    pre_act = jnp.einsum(
        "iwjv,najbvd->naibwd", mix_table, window_tiles, preferred_element_type=jnp.float32
    )
    pre_act = pre_act.reshape(item_count, lat_rows, block_width, feature_dim)
    mixed_out = (tokens.astype(jnp.float32) + gelu_exact(pre_act)).astype(jnp.bfloat16)
    return (mixed_out, pre_act)


def window_backward(grad_out, pre_act, mix_table):
    item_count, lat_rows, block_width, feature_dim = grad_out.shape
    grad_float = grad_out.astype(jnp.float32)
    grad_pre = jax.vjp(gelu_exact, pre_act)[1](grad_float)[0].astype(jnp.bfloat16)
    grad_tiles = grad_pre.reshape(
        item_count, lat_rows // WLAT, WLAT, block_width // WLON, WLON, feature_dim
    )
    spread = jnp.einsum(
        "iwjv,naibwd->najbvd", mix_table, grad_tiles, preferred_element_type=jnp.float32
    )
    spread = spread.reshape(item_count, lat_rows, block_width, feature_dim)
    return (grad_float + spread).astype(jnp.bfloat16)


def weight_gradient(pixels, grad_tokens, level_merge_weight):
    grad_embed = jnp.einsum(
        "nte,lde->nltd", grad_tokens, level_merge_weight, preferred_element_type=jnp.float32
    ).astype(jnp.bfloat16)
    return jnp.einsum("nlkt,nltd->kd", pixels, grad_embed, preferred_element_type=jnp.float32)


def on_device(
    patches,
    variable_group_index,
    frozen_patch_weight,
    adapter_down,
    adapter_up,
    level_merge_weight,
    window_patch_mixer,
    column_block_owner,
    mixed_token_gradient,
):
    full_a, full_b = (
        lax.all_gather(adapter_down, "rep", axis=0, tiled=True),
        lax.all_gather(adapter_up, "rep", axis=1, tiled=True),
    )
    groups = frozen_patch_weight.shape[0]
    feature_dim = frozen_patch_weight.shape[2]
    selector = (
        variable_group_index[:, None] == jnp.arange(groups, dtype=jnp.int32)[None, :]
    ).astype(jnp.float32)
    base_rows = jnp.einsum(
        "vg,gad->vad", selector, frozen_patch_weight.astype(jnp.float32)
    ).reshape(-1, feature_dim)
    merged = (base_rows + jnp.dot(full_a, full_b, preferred_element_type=jnp.float32)).astype(
        jnp.bfloat16
    )
    band_count = lax.axis_size("band")
    samples, level_stack, channels, row_count, col_count = patches.shape
    block_width = col_count // band_count
    lat_rows = band_count * row_count
    block_ids = jnp.arange(band_count, dtype=jnp.int32)
    inverse = jnp.sum(
        jnp.where(column_block_owner[None, :] == block_ids[:, None], block_ids[None, :], 0), axis=1
    )
    mix_table = window_patch_mixer.reshape(WLAT, WLON, WLAT, WLON)
    grad_window = mixed_token_gradient.reshape(samples, lat_rows, block_width, feature_dim)
    pixels = patches.reshape(samples, level_stack, channels, row_count * col_count)
    tokens = embed_tokens(pixels, merged, level_merge_weight)
    blocks = tokens.reshape(samples, row_count, band_count, block_width, feature_dim)
    outgoing = jnp.take(blocks, inverse, axis=2)
    arrived = lax.all_to_all(outgoing, "band", split_axis=2, concat_axis=1, tiled=True)
    item_count = arrived.shape[0]
    flat_tokens = arrived.reshape(item_count, arrived.shape[1], block_width, feature_dim)
    mixed_out, pre_act = window_forward(flat_tokens, mix_table)
    mixed_out, pre_act = (
        mixed_out.reshape(item_count, 1, arrived.shape[1], block_width, feature_dim),
        pre_act,
    )
    grad_tokens = window_backward(grad_window, pre_act, mix_table)
    returned = lax.all_to_all(
        grad_tokens.reshape(samples, lat_rows, 1, block_width, feature_dim),
        "band",
        split_axis=1,
        concat_axis=2,
        tiled=True,
    )
    ordered = jnp.take(returned, column_block_owner, axis=2).reshape(
        samples, row_count * col_count, feature_dim
    )
    local_grad = weight_gradient(pixels, ordered, level_merge_weight)
    factor_b = full_b.astype(jnp.float32)
    factor_a = full_a.astype(jnp.float32)
    summed = lax.psum(local_grad, ("band", "rep"))
    rep_index = lax.axis_index("rep")
    row_share = summed.shape[0] // lax.axis_size("rep")
    col_share = summed.shape[1] // lax.axis_size("rep")
    rows_part = lax.dynamic_slice_in_dim(summed, rep_index * row_share, row_share, 0)
    cols_part = lax.dynamic_slice_in_dim(summed, rep_index * col_share, col_share, 1)
    first_factor_gradient = jnp.dot(rows_part, factor_b.T, precision=lax.Precision.HIGHEST)
    second_factor_gradient = jnp.dot(factor_a.T, cols_part, precision=lax.Precision.HIGHEST)
    return (mixed_out, first_factor_gradient, second_factor_gradient)


def solution(mesh):
    in_specs = (
        P("rep", None, None, "band", None),
        P(),
        P(),
        P("rep", None),
        P(None, "rep"),
        P(),
        P(),
        P(),
        P("rep", "band", None, None, None),
    )
    out_specs = (P("rep", "band", None, None, None), P("rep", None), P(None, "rep"))
    return jax.shard_map(
        on_device, mesh=mesh, in_specs=in_specs, out_specs=out_specs, check_vma=False
    )
```

profile of v0, /device:TPU:1, one launch (start us, length us, event | category | flops | bytes accessed | tf_op | source)
XLA Modules:
  0.0 452.7 jit_solution(6002257955842975513)
XLA Ops:
  7.2 0.0 copy-start
  7.2 0.9 select_reduce_fusion
  8.1 9.6 %all_gather.7 = bf16[16,512]{1,0:T(8,128)(2,1)S(1)} all-gather(bf16[16,128]{1,0:T(8,128)(2,1)} %param.15), channel_id=1, replica_groups=mesh['band'=64,'rep'=4] {'rep'}, dimensions={1}, use_global_device_ids=true | all-gather | bytes 20480 | tf_op jit(solution)/shard_map/all_gather | solution.py:70
  17.8 9.2 %all-gather = bf16[4,20,16]{1,2,0:T(8,128)(2,1)S(1)} all-gather(bf16[1,20,16]{1,2,0:T(8,128)(2,1)} %bitcast.205), channel_id=1, replica_groups=mesh['band'=64,'rep'=4] {'rep'}, dimensions={0}, use_global_device_ids=true | all-gather | bytes 3200 | tf_op jit(solution)/shard_map/all_gather | solution.py:69
  26.9 0.1 reshape.357
  27.0 1.0 fusion.73
  28.1 0.1 copy.86
  28.2 0.2 fusion.68
  28.4 0.0 copy-done
  28.4 7.4 %bitcast_convert_fusion = bf16[2,768,512]{2,1,0:T(8,128)(2,1)} fusion(bf16[4,512,512]{2,1,0:T(8,128)(2,1)S(1)} %copy-done, bf16[80,512,1,1]{1,0,3,2:T(8,128)(2,1)S(1)} %fusion.68, bf16[2,4,80,1,768]{4,2,3,1,0:T(8,128)(2,1)} %param.11), kind=kOutput, calls=%fused_computation.51 | convolution fusion | flops 3728474112 | bytes 4734976 | tf_op jit(solution)/shard_map/nltd,lde->nte/dot_general | solution.py:18
  35.8 4.2 copy.89
  40.0 6.2 %gather_fusion = bf16[64,2,12,512]{3,1,2,0:T(2,128)(2,1)} fusion(bf16[2,64,12,512]{3,0,2,1:T(2,128)(2,1)} %bitcast.199, s32[1024]{0:T(1024)S(1)} %pad_clamp_fusion.1), kind=kCustom, calls=%fused_computation.clone | custom fusion | bytes 3145984 | tf_op jit(solution)/shard_map/jit(_take)/gather | solution.py:96
  46.2 0.0 copy-start.4
  46.2 4.1 fusion.59
  50.2 18.1 %all-to-all-start = ((bf16[2,1,64,12,512]{4,0,3,1,2:T(2,128)(2,1)}), bf16[2,1,64,12,512]{4,0,3,1,2:T(2,128)(2,1)}, u32[]{:S(2)}, u32[]{:S(2)}) async-start(bf16[2,1,64,12,512]{4,0,3,1,2:T(2,128)(2,1)} %fusion.59), calls=%async_computation | async-start | bytes 3145728 | tf_op jit(solution)/shard_map/all_to_all | solution.py:97
  68.3 0.0 copy-done.4
  68.3 0.2 reshape.328
  68.5 3.5 convert_bitcast_fusion
  72.0 35.8 %all-to-all-done = bf16[2,1,64,12,512]{4,0,3,1,2:T(2,128)(2,1)} async-done(((bf16[2,1,64,12,512]{4,0,3,1,2:T(2,128)(2,1)}), bf16[2,1,64,12,512]{4,0,3,1,2:T(2,128)(2,1)}, u32[]{:S(2)}, u32[]{:S(2)}) %all-to-all-start) | async-done | bytes 1572896 | tf_op jit(solution)/shard_map/all_to_all | solution.py:97
  107.8 1.8 copy.92
  109.7 0.0 copy-start.3
  109.7 0.8 fusion.71
  110.5 0.0 copy-start.2
  110.5 2.0 copy-done.2
  112.5 0.0 copy-done.3
  112.5 0.0 copy-start.1
  112.5 22.6 %convolution_bitcast_fusion = f32[2,8,8,1,12,512]{5,4,2,1,0,3:T(8,128)S(1)} fusion(f32[2,8,8,1,12,512]{5,2,1,4,0,3:T(8,128)S(1)} %copy-done.3, bf16[8,12,8,12,1,1]{3,2,1,0,5,4:T(8,128)(2,1)S(1)} %bitcast.204, f32[2,8,512,8,12,1]{2,4,5,3,1,0:T(8,128)S(1)} %fusion.71), kind=kOutput, calls=%fused_computation.68 | convolution fusion | flops 207618048 | bytes 9455616 | tf_op jit(solution)/shard_map/iwjv,naibwd->najbvd/dot_general | solution.py:43
  135.0 0.0 copy-done.1
  135.1 2.0 fusion.25
  137.0 0.0 copy-start.6
  137.0 2.8 copy.100
  139.8 6.3 %all-to-all-start.1 = ((bf16[2,64,1,12,512]{4,0,3,2,1:T(2,128)(2,1)}), bf16[2,64,1,12,512]{4,0,3,2,1:T(2,128)(2,1)}, u32[]{:S(2)}, u32[]{:S(2)}) async-start(bf16[2,64,1,12,512]{4,0,3,2,1:T(2,128)(2,1)} %copy.100), calls=%async_computation.1 | async-start | bytes 3145728 | tf_op jit(solution)/shard_map/all_to_all | solution.py:106
  146.1 0.0 all-reduce.2.cloned.1.call-start
  146.1 0.0 copy-done.6
  146.2 7.0 %fusion.16 = (f32[2,8,8,1,12,512]{5,4,2,1,0,3:T(8,128)}, f32[2,8,8,1,12,512]{5,4,2,1,0,3:T(8,128)}) fusion(f32[2,8,512,8,12,1]{2,4,5,3,1,0:T(8,128)} %copy-done.2), kind=kLoop, calls=%fused_computation.24 | loop fusion | flops 2359296 | bytes 9437184 | tf_op jit(solution)/shard_map/mul | solution.py:11
  153.2 32.6 %all-to-all-done.1 = bf16[2,64,1,12,512]{4,0,3,2,1:T(2,128)(2,1)} async-done(((bf16[2,64,1,12,512]{4,0,3,2,1:T(2,128)(2,1)}), bf16[2,64,1,12,512]{4,0,3,2,1:T(2,128)(2,1)}, u32[]{:S(2)}, u32[]{:S(2)}) %all-to-all-start.1) | async-done | bytes 1572896 | tf_op jit(solution)/shard_map/all_to_all | solution.py:106
  185.8 0.0 copy-start.5
  185.8 6.2 %gather_fusion.1 = bf16[64,2,12,512]{3,1,2,0:T(2,128)(2,1)} fusion(bf16[2,64,12,512]{3,0,2,1:T(2,128)(2,1)} %bitcast.41, s32[1024]{0:T(1024)S(1)} %pad_clamp_fusion), kind=kCustom, calls=%fused_computation.1.clone | custom fusion | bytes 3145984 | tf_op jit(solution)/shard_map/jit(_take)/gather | solution.py:113
  192.1 4.1 broadcast_select_fusion
  196.1 0.0 copy-done.5
  196.1 6.6 %fusion.60 = f32[80,512]{1,0:T(8,128)} fusion(bf16[4,512,512]{2,1,0:T(8,128)(2,1)S(1)} %copy-done, bf16[2,768,512]{2,0,1:T(2,128)(2,1)} %bitcast.201, bf16[2,4,80,1,768]{4,2,3,1,0:T(8,128)(2,1)S(1)} %copy-done.5), kind=kOutput, calls=%fused_computation.75 | convolution fusion | flops 3727687680 | bytes 4816896 | tf_op jit(solution)/shard_map/nlkt,nltd->kd/dot_general | solution.py:54
  202.8 0.0 all-reduce.2.cloned.1.call-update
  202.8 11.2 %fusion.29 = bf16[2,1,64,12,512]{4,2,3,1,0:T(8,128)(2,1)} fusion(f32[2,8,8,1,12,512]{5,4,2,1,0,3:T(8,128)} %get-tuple-element.14, f32[2,8,8,1,12,512]{5,4,2,1,0,3:T(8,128)} %get-tuple-element.13, bf16[2,1,64,12,512]{4,0,3,1,2:T(2,128)(2,1)} %all-to-all-done), kind=kLoop, calls=%fused_computation.45 | loop fusion | flops 50331648 | bytes 9437184 | tf_op jit(solution)/shard_map/convert_element_type | solution.py:32
  214.0 228.6 %all-reduce.2.cloned.1.call-done = f32[80,512]{1,0:T(8,128)} async-done(((f32[80,512]{1,0:T(8,128)}), f32[80,512]{1,0:T(8,128)}) %all-reduce.2.cloned.1.call-update) | async-done | bytes 163856 | tf_op jit(solution)/shard_map/psum | solution.py:119
  442.6 1.6 fusion.75
  444.2 1.5 convolution_bitcast_fusion.1
  (7 shorter events, 0.0 us)
Async XLA Ops:
  7.2 21.2 %copy-start = (bf16[4,512,512]{2,1,0:T(8,128)(2,1)S(1)}, bf16[4,512,512]{2,1,0:T(8,128)(2,1)}, u32[]{:S(2)}) copy-start(bf16[4,512,512]{2,1,0:T(8,128)(2,1)} %param.16) | copy-start | bytes 6291460
  46.2 22.2 %copy-start.4 = (bf16[96,96]{1,0:T(8,128)(2,1)S(1)}, bf16[96,96]{1,0:T(8,128)(2,1)}, u32[]{:S(2)}) copy-start(bf16[96,96]{1,0:T(8,128)(2,1)} %param.17) | copy-start | bytes 55300
  50.2 57.6 %all-to-all-start = ((bf16[2,1,64,12,512]{4,0,3,1,2:T(2,128)(2,1)}), bf16[2,1,64,12,512]{4,0,3,1,2:T(2,128)(2,1)}, u32[]{:S(2)}, u32[]{:S(2)}) async-start(bf16[2,1,64,12,512]{4,0,3,1,2:T(2,128)(2,1)} %fusion.59), calls=%async_computation | async-start | bytes 3145728 | tf_op jit(solution)/shard_map/all_to_all | solution.py:97
  109.7 2.8 copy-start.3
  110.5 2.0 copy-start.2
  112.5 22.6 %copy-start.1 = (bf16[2,1,64,12,512]{4,2,3,1,0:T(8,128)(2,1)S(1)}, bf16[2,1,64,12,512]{4,2,3,1,0:T(8,128)(2,1)}, u32[]{:S(2)}) copy-start(bf16[2,1,64,12,512]{4,2,3,1,0:T(8,128)(2,1)} %param.19) | copy-start | bytes 4718596
  137.0 9.1 %copy-start.6 = (s32[64]{0:T(128)S(1)}, s32[64]{0:T(128)}, u32[]{:S(2)}) copy-start(s32[64]{0:T(128)} %param.18) | copy-start | bytes 772
  139.8 46.0 %all-to-all-start.1 = ((bf16[2,64,1,12,512]{4,0,3,2,1:T(2,128)(2,1)}), bf16[2,64,1,12,512]{4,0,3,2,1:T(2,128)(2,1)}, u32[]{:S(2)}, u32[]{:S(2)}) async-start(bf16[2,64,1,12,512]{4,0,3,2,1:T(2,128)(2,1)} %copy.100), calls=%async_computation.1 | async-start | bytes 3145728 | tf_op jit(solution)/shard_map/all_to_all | solution.py:106
  146.1 296.5 %all-reduce.2.cloned.1.call-start = ((), (), s32[]{:S(2)}) async-start(), calls=%async_computation.2 | async-start | bytes 327680 | tf_op jit(solution)/shard_map/psum | solution.py:119
  185.8 10.3 %copy-start.5 = (bf16[2,4,80,1,768]{4,2,3,1,0:T(8,128)(2,1)S(1)}, bf16[2,4,80,1,768]{4,2,3,1,0:T(8,128)(2,1)}, u32[]{:S(2)}) copy-start(bf16[2,4,80,1,768]{4,2,3,1,0:T(8,128)(2,1)} %param.11) | copy-start | bytes 2949124
Sparse Core Ops, SparseCore 0:
  202.9 239.6 all-reduce.1
where the time goes:
time: 457 us; the launch traced here: 453 us
  waiting for transfers between devices  297 us (65%)
  matrix products  41.8 us (9%)
  other arithmetic  32.7 us (7%)
  starting transfers between devices  24.4 us (5%)
  local copies, waits for them, and re-layouts  23.5 us (5%)
  blocking collectives  18.8 us (4%)
  between operations  14.4 us (3%)
    psum x1, waiting for transfers between devices, on_device(): summed = lax.psum(local_grad, ('band', 'rep'))  229 us
    all_to_all x1, waiting for transfers between devices, on_device(): lax.all_to_all(outgoing, 'band', split_axis=2, concat_axis=1, tiled=True)  35.8 us
    all_to_all x1, waiting for transfers between devices, on_device(): lax.all_to_all(grad_tokens.reshape(samples, lat_rows, 1, block_width, fea...  32.6 us
    dot_general x1, matrix products, window_backward(): jnp.einsum('iwjv,naibwd->najbvd', mix_table, grad_tiles, preferred_elemen...  22.6 us
    all_to_all x1, starting transfers between devices, on_device(): lax.all_to_all(outgoing, 'band', split_axis=2, concat_axis=1, tiled=True)  18.1 us
    convert_element_type x1, other arithmetic, window_forward(): (tokens.astype(jnp.float32) + gelu_exact(pre_act)).astype(jnp.bfloat16)  11.2 us
    all_gather x1, blocking collectives, on_device(): lax.all_gather(adapter_up, 'rep', axis=1, tiled=True)  9.63 us
    all_gather x1, blocking collectives, on_device(): lax.all_gather(adapter_down, 'rep', axis=0, tiled=True)  9.17 us
  transfers between devices with their start and end apart: 3, of which 3 were waited for; matrix products, arithmetic and copies ran while one was open for 5% of the time, Pallas kernels for 0%

commit v1 on v0

v1 whole, which is shorter than its diff:
```python
import jax
import jax.numpy as jnp
import numpy as np
from jax import lax
from jax.experimental import pallas as pl
from jax.experimental.pallas import tpu as pltpu
from jax.sharding import PartitionSpec as P

WLAT = 8
WLON = 12
MESH = pl.DeviceIdType.MESH
F32 = jnp.float32
BF16 = jnp.bfloat16
NT = (((1,), (1,)), ((), ()))
TN = (((0,), (0,)), ((), ()))
CHUNK = 16


def dot(a, b, dims=(((1,), (0,)), ((), ()))):
    return lax.dot_general(a, b, dims, preferred_element_type=F32)


ROWS = [(0, w) for w in range(8)] + [(1, w) for w in range(8)]
ROWS += [(0, w) for w in range(8, 12)] + [(1, w) for w in range(8, 12)]


def window_constants():
    pick = np.zeros((192, 96), np.float32)
    sample = np.zeros((192,), np.int32)
    for r in range(8):
        for u, (n, w) in enumerate(ROWS):
            pick[r * 24 + u, r * 12 + w] = 1
            sample[r * 24 + u] = n
    same = (sample[:, None] == sample[None, :]).astype(np.float32)
    return jnp.asarray(pick, BF16), jnp.asarray(same, F32)


def kernel(
    patches, vgi, frozen, down_t, up, level_w, mixer, owner, grad, pick, same,
    mixed, first_t, second,
    px, px2, wv, gv, send, recv, merge_m, mix_f, mix_b, down_all, up_all,
    pre_v, tok_v, gd_v, gp_v, pk_v, mo, xacc, xb, st1, rb1, st2, rb2, rb3,
    in_sem, send_sem, recv_sem, ad_send, ad_recv, out_sem, red_send, red_recv,
):
    me = lax.axis_index("band")
    rep = lax.axis_index("rep")
    group = me // 8

    load_p = pltpu.make_async_copy(patches, px, in_sem.at[0])
    load_w = pltpu.make_async_copy(level_w, wv, in_sem.at[1])
    load_g = pltpu.make_async_copy(grad, gv, in_sem.at[2])
    load_p.start()
    load_w.start()
    load_g.start()

    barrier = pltpu.get_barrier_semaphore()

    def greet(e, _):
        pl.semaphore_signal(barrier, inc=1, device_id={"band": me ^ e}, device_id_type=MESH)
        return 0

    lax.fori_loop(1, 64, greet, 0)
    for i in range(1, 4):
        pl.semaphore_signal(
            barrier, inc=1, device_id={"rep": lax.rem(rep + i, 4)}, device_id_type=MESH
        )

    down_all[rep] = jnp.zeros((16, 128), BF16)
    down_all[rep, :, 0:20] = down_t[...]
    up_all[rep] = up[...]

    jj = lax.broadcasted_iota(jnp.int32, (64, 768), 0)
    tt = lax.broadcasted_iota(jnp.int32, (64, 768), 1)
    block_of = jnp.where((tt >= jj * 12) & (tt < jj * 12 + 12), 1.0, 0.0).astype(BF16)
    own8 = jnp.broadcast_to(owner[...].astype(F32), (8, 64)).astype(BF16)
    num8 = lax.broadcasted_iota(jnp.int32, (8, 64), 1).astype(F32).astype(BF16)
    t8 = lax.broadcasted_iota(jnp.int32, (8, 768), 1).astype(F32)
    key = dot(own8, block_of) * 16.0 + t8 - 12.0 * dot(num8, block_of)
    key = key.astype(jnp.int32)[0:1, :]

    load_p.wait()
    px2[0:64, :] = px[0, 256:320, :]
    px2[64:128, :] = px[1, 256:320, :]

    pl.semaphore_wait(barrier, 66)

    def adapters(i):
        peer = {"rep": lax.rem(rep + i, 4)}
        return (
            pltpu.make_async_remote_copy(
                down_all.at[rep], down_all.at[rep], ad_send.at[0], ad_recv.at[0],
                device_id=peer, device_id_type=MESH,
            ),
            pltpu.make_async_remote_copy(
                up_all.at[rep], up_all.at[rep], ad_send.at[1], ad_recv.at[1],
                device_id=peer, device_id_type=MESH,
            ),
        )

    for i in range(1, 4):
        for copy in adapters(i):
            copy.start()

    def pack(c, _):
        row = lax.broadcasted_iota(jnp.int32, (CHUNK * 16, 768), 0)
        rr = row & 15
        slot = c * CHUNK + lax.shift_right_logical(row, 4)
        want = (slot ^ me) * 16 + jnp.where(rr < 12, rr, rr - 4)
        z = jnp.where(want == key, 1.0, 0.0).astype(BF16)
        d0 = dot(z, px[0, 0:256, :], NT).reshape(CHUNK, 16, 256)
        d1 = dot(z, px[1, 0:256, :], NT).reshape(CHUNK, 16, 256)
        d2 = dot(z, px2[...], NT).reshape(CHUNK, 16, 128)
        low = lax.broadcasted_iota(jnp.int32, (CHUNK, 8, 256), 1) < 4
        parts = [
            d0[:, 0:8],
            d1[:, 0:8],
            jnp.where(low, d0[:, 8:16], d1[:, 8:16]),
            jnp.concatenate([d2[:, 0:8], d2[:, 8:16]], axis=2),
        ]
        send[pl.ds(c * CHUNK, CHUNK)] = jnp.concatenate(parts, axis=1).astype(BF16)

        def ship(i, _):
            e = c * CHUNK + i

            @pl.when(e != 0)
            def _():
                pltpu.make_async_remote_copy(
                    send.at[e], recv.at[me], send_sem, recv_sem.at[group],
                    device_id={"band": me ^ e}, device_id_type=MESH,
                ).start()

            @pl.when(e == 0)
            def _():
                pltpu.make_async_copy(send.at[0], recv.at[me], recv_sem.at[group]).start()

            return 0

        lax.fori_loop(0, CHUNK, ship, 0)
        return 0

    lax.fori_loop(0, 64 // CHUNK, pack, 0)

    pltpu.make_async_copy(down_all.at[0:3], down_all.at[0:3], ad_recv.at[0]).wait()
    pltpu.make_async_copy(up_all.at[0:3], up_all.at[0:3], ad_recv.at[1]).wait()
    down_f = down_all[0].astype(F32)
    for i in range(1, 4):
        down_f += pltpu.roll(down_all[i].astype(F32), 20 * i, 1)
    down_b = down_f.astype(BF16)
    up_b = jnp.concatenate([up_all[i] for i in range(4)], axis=1)
    base = jnp.concatenate([frozen[vgi[v]].astype(F32) for v in range(5)], axis=0)
    merged = (base + dot(down_b, up_b, TN)[0:80]).astype(BF16)
    load_w.wait()
    for l in range(4):
        merge_m[80 * l : 80 * l + 80, :] = dot(merged, wv[l]).astype(BF16)
    merge_m[320:384, :] = merge_m[256:320, :]

    half = dot(pick[...], mixer[...]).astype(BF16)
    mix_f[...] = (dot(half, pick[...], NT) * same[...]).astype(BF16)
    half_t = dot(pick[...], mixer[...], (((1,), (1,)), ((), ()))).astype(BF16)
    mix_b[...] = (dot(half_t, pick[...], NT) * same[...]).astype(BF16)

    xacc[...] = jnp.zeros((384, 512), F32)
    load_g.wait()

    def out_copy(step, a):
        slot = step & 1
        return pltpu.make_async_copy(
            mo.at[slot], mixed.at[:, pl.ds(a * 8, 8)], out_sem.at[slot]
        )

    def windows(step, _):
        a = group ^ step
        here = recv.at[pl.ds(a * 8, 8)]
        pltpu.make_async_copy(here, here, recv_sem.at[a]).wait()

        @pl.when(step >= 2)
        def _():
            out_copy(step, a).wait()

        got = recv[pl.ds(a * 8, 8)].astype(F32)
        pk_v[:, 0:256] = got[:, 0:24].reshape(192, 256).astype(BF16)
        left = lax.broadcasted_iota(jnp.int32, (8, 8, 128), 2) < 64
        up4 = lax.broadcasted_iota(jnp.int32, (8, 8, 128), 1) < 4
        t0, t1 = got[:, 24:32, 0:128], got[:, 24:32, 128:256]
        zero = jnp.zeros((8, 8, 128), F32)
        tail = jnp.concatenate(
            [
                jnp.where(left, t0, zero),
                jnp.where(left, zero, t0),
                jnp.where(left == up4, t1, zero),
            ],
            axis=1,
        )
        pk_v[:, 256:384] = tail.reshape(192, 128).astype(BF16)
        tok = dot(pk_v[...], merge_m[...]).astype(BF16)
        tok_v[...] = tok.astype(F32)
        pre_v[...] = dot(mix_f[...], tok)

        slot = step & 1
        for i in range(4):
            g0 = gv[0, pl.ds(a * 8 + 2 * i, 2)].astype(F32)
            g1 = gv[1, pl.ds(a * 8 + 2 * i, 2)].astype(F32)
            g = jnp.concatenate(
                [g0[:, 0:8], g1[:, 0:8], g0[:, 8:12], g1[:, 8:12]], axis=1
            ).reshape(48, 512)
            x = pre_v[48 * i : 48 * i + 48, :]
            cdf = 0.5 * (1.0 + lax.erf(x * np.float32(2**-0.5)))
            pdf = jnp.exp(-0.5 * x * x) * np.float32((2 * np.pi) ** -0.5)
            m = (tok_v[48 * i : 48 * i + 48, :] + x * cdf).reshape(2, 24, 512)
            gd_v[48 * i : 48 * i + 48, :] = g
            gp_v[48 * i : 48 * i + 48, :] = (g * (cdf + x * pdf)).astype(BF16)
            m0 = jnp.concatenate([m[:, 0:8], m[:, 16:20]], axis=1)
            m1 = jnp.concatenate([m[:, 8:16], m[:, 20:24]], axis=1)
            mo[slot, 0, 2 * i : 2 * i + 2] = m0.astype(BF16)
            mo[slot, 1, 2 * i : 2 * i + 2] = m1.astype(BF16)
        out_copy(step, a).start()
        grad_tok = (gd_v[...] + dot(mix_b[...], gp_v[...])).astype(BF16)
        xacc[...] += dot(pk_v[...], grad_tok, TN)
        return 0

    lax.fori_loop(0, 8, windows, 0)

    xb[0:256, :] = xacc[0:256, :].astype(BF16)
    xb[256:320, :] = (xacc[256:320, :] + xacc[320:384, :]).astype(BF16)
    wg = dot(xb[0:80, :], wv[0], NT)
    for l in range(1, 4):
        wg += dot(xb[80 * l : 80 * l + 80, :], wv[l], NT)
    wgb = wg.astype(BF16)
    sec = dot(down_b[:, 0:80], wgb)
    fst = dot(up_b, wgb, NT)
    for i in range(4):
        st1[i, 0:16, :] = sec[:, 128 * i : 128 * i + 128]
        st1[i, 16:32, :] = jnp.zeros((16, 128), F32)
        st1[i, 16:32, 0:80] = fst

    z = lax.rem(me // 2, 8)
    xc = (me // 16) * 2 + lax.rem(me, 2)

    rb1[rep] = st1[rep]
    for i in range(1, 4):
        to = lax.rem(rep + i, 4)
        pltpu.make_async_remote_copy(
            st1.at[to], rb1.at[rep], red_send.at[0], red_recv.at[0],
            device_id={"rep": to}, device_id_type=MESH,
        ).start()
    pltpu.make_async_copy(rb1.at[0:3], rb1.at[0:3], red_recv.at[0]).wait()
    st2[0] = rb1[0] + rb1[1] + rb1[2] + rb1[3]

    rb2[xc] = st2[0]
    for j in range(1, 8):
        to = xc ^ j
        pltpu.make_async_remote_copy(
            st2.at[0], rb2.at[xc], red_send.at[1], red_recv.at[1],
            device_id={"band": (to // 2) * 16 + z * 2 + lax.rem(to, 2)}, device_id_type=MESH,
        ).start()
    pltpu.make_async_copy(rb2.at[0:7], rb2.at[0:7], red_recv.at[1]).wait()
    total = rb2[0]
    for j in range(1, 8):
        total += rb2[j]
    st2[1] = total

    rb3[z] = st2[1]
    for j in range(1, 8):
        to = z ^ j
        pltpu.make_async_remote_copy(
            st2.at[1], rb3.at[z], red_send.at[2], red_recv.at[2],
            device_id={"band": (me // 16) * 16 + to * 2 + lax.rem(me, 2)}, device_id_type=MESH,
        ).start()
    pltpu.make_async_copy(rb3.at[0:7], rb3.at[0:7], red_recv.at[2]).wait()
    total = rb3[0]
    for j in range(1, 8):
        total += rb3[j]
    second[...] = total[0:16]
    first_t[...] = pltpu.roll(total[16:32], lax.rem(128 - 20 * rep, 128), 1)[:, 0:20]

    out_copy(6, group).wait()
    out_copy(7, group).wait()
    pltpu.make_async_copy(send.at[1:64], send.at[1:64], send_sem).wait()
    pltpu.make_async_copy(down_all.at[0:3], down_all.at[0:3], ad_send.at[0]).wait()
    pltpu.make_async_copy(up_all.at[0:3], up_all.at[0:3], ad_send.at[1]).wait()
    pltpu.make_async_copy(rb1.at[0:3], rb1.at[0:3], red_send.at[0]).wait()
    pltpu.make_async_copy(rb2.at[0:7], rb2.at[0:7], red_send.at[1]).wait()
    pltpu.make_async_copy(rb3.at[0:7], rb3.at[0:7], red_send.at[2]).wait()


def on_device(
    patches,
    variable_group_index,
    frozen_patch_weight,
    adapter_down,
    adapter_up,
    level_merge_weight,
    window_patch_mixer,
    column_block_owner,
    mixed_token_gradient,
):
    pick, same = window_constants()
    vmem = pl.BlockSpec(memory_space=pltpu.VMEM)
    smem = pl.BlockSpec(memory_space=pltpu.SMEM)
    hbm = pl.BlockSpec(memory_space=pl.ANY)
    dma = pltpu.SemaphoreType.DMA
    mixed, first_t, second = pl.pallas_call(
        kernel,
        out_shape=(
            jax.ShapeDtypeStruct((2, 64, 12, 512), BF16),
            jax.ShapeDtypeStruct((16, 20), F32),
            jax.ShapeDtypeStruct((16, 128), F32),
        ),
        in_specs=[hbm, smem, vmem, vmem, vmem, hbm, vmem, vmem, hbm, vmem, vmem],
        out_specs=(hbm, vmem, vmem),
        scratch_shapes=[
            pltpu.VMEM((2, 320, 768), BF16),
            pltpu.VMEM((128, 768), BF16),
            pltpu.VMEM((4, 512, 512), BF16),
            pltpu.VMEM((2, 64, 12, 512), BF16),
            pltpu.VMEM((64, 32, 256), BF16),
            pltpu.VMEM((64, 32, 256), BF16),
            pltpu.VMEM((384, 512), BF16),
            pltpu.VMEM((192, 192), BF16),
            pltpu.VMEM((192, 192), BF16),
            pltpu.VMEM((4, 16, 128), BF16),
            pltpu.VMEM((4, 16, 128), BF16),
            pltpu.VMEM((192, 512), F32),
            pltpu.VMEM((192, 512), F32),
            pltpu.VMEM((192, 512), F32),
            pltpu.VMEM((192, 512), BF16),
            pltpu.VMEM((192, 384), BF16),
            pltpu.VMEM((2, 2, 8, 12, 512), BF16),
            pltpu.VMEM((384, 512), F32),
            pltpu.VMEM((320, 512), BF16),
            pltpu.VMEM((4, 32, 128), F32),
            pltpu.VMEM((4, 32, 128), F32),
            pltpu.VMEM((2, 32, 128), F32),
            pltpu.VMEM((8, 32, 128), F32),
            pltpu.VMEM((8, 32, 128), F32),
            dma((3,)),
            dma,
            dma((8,)),
            dma((2,)),
            dma((2,)),
            dma((2,)),
            dma((3,)),
            dma((3,)),
        ],
        compiler_params=pltpu.CompilerParams(
            collective_id=0, has_side_effects=True, vmem_limit_bytes=48 << 20
        ),
        name="patch_window_kernel",
    )(
        patches.reshape(2, 320, 768),
        variable_group_index,
        frozen_patch_weight,
        adapter_down.T,
        adapter_up,
        level_merge_weight,
        window_patch_mixer,
        column_block_owner.reshape(1, 64),
        mixed_token_gradient.reshape(2, 64, 12, 512),
        pick,
        same,
    )
    return (mixed.reshape(2, 1, 64, 12, 512), first_t.T, second)


def solution(mesh):
    in_specs = (
        P("rep", None, None, "band", None),
        P(),
        P(),
        P("rep", None),
        P(None, "rep"),
        P(),
        P(),
        P(),
        P("rep", "band", None, None, None),
    )
    out_specs = (P("rep", "band", None, None, None), P("rep", None), P(None, "rep"))
    return jax.shard_map(
        on_device, mesh=mesh, in_specs=in_specs, out_specs=out_specs, check_vma=False
    )
```

time: 457 us -> 64.8 us (0.14)
  waiting for transfers between devices: 297 us -> 0 us
  Pallas kernels: 0 us -> 56.9 us
  matrix products: 41.8 us -> 0 us
  other arithmetic: 32.7 us -> 0 us
  starting transfers between devices: 24.4 us -> 0 us
  blocking collectives: 18.8 us -> 0 us
  local copies, waits for them, and re-layouts: 23.5 us -> 7.06 us
  between operations: 14.4 us -> 0.78 us
    psum x1 -> x0, waiting for transfers between devices: 229 us -> none  [on_device(): summed = lax.psum(local_grad, ('band', 'rep'))]
    all_to_all x2 -> x0, waiting for transfers between devices: 68.5 us -> none  [the longest x1 35.8 us: on_device(): lax.all_to_all(outgoing, 'band', split_axis=2, concat_axis=1, tiled=True)]
    pallas_call x0 -> x1, Pallas kernels: none -> 56.9 us  [on_device(): pl.pallas_call(kernel, out_shape=(jax.ShapeDtypeStruct((2, 64, 12, 512),...]
    dot_general x8 -> x0, matrix products: 41.8 us -> none  [the longest x1 22.6 us: window_backward(): jnp.einsum('iwjv,naibwd->najbvd', mix_table, grad_tiles, preferred_elemen...]
    all_to_all x2 -> x0, starting transfers between devices: 24.4 us -> none  [the longest x1 18.1 us: on_device(): lax.all_to_all(outgoing, 'band', split_axis=2, concat_axis=1, tiled=True)]
    all_gather x2 -> x0, blocking collectives: 18.8 us -> none  [the longest x1 9.63 us: on_device(): lax.all_gather(adapter_up, 'rep', axis=1, tiled=True)]
    convert_element_type x3 -> x0, other arithmetic: 16.6 us -> none  [the longest x1 11.2 us: window_forward(): (tokens.astype(jnp.float32) + gelu_exact(pre_act)).astype(jnp.bfloat16)]
    gather x2 -> x0, local copies, waits for them, and re-layouts: 12.4 us -> none  [the longest x1 6.24 us: on_device(): jnp.take(returned, column_block_owner, axis=2)]
  transfers between devices with their start and end apart: 3 -> 0, of which waited for: 3 -> 0; matrix products, arithmetic and copies ran while one was open for 5% -> 0% of each run, Pallas kernels for 0% -> 0%
where the time goes in v1:
time: 64.8 us; the launch traced here: 64.7 us
  Pallas kernels  56.9 us (88%)
  local copies, waits for them, and re-layouts  7.06 us (11%)
  between operations  0.78 us (1%)
    pallas_call x1, Pallas kernels, on_device(): pl.pallas_call(kernel, out_shape=(jax.ShapeDtypeStruct((2, 64, 12, 512),...  56.9 us
    unnamed x24, local copies, waits for them, and re-layouts  7.06 us

profile of v1, /device:TPU:1, one launch (start us, length us, event | category | flops | bytes accessed | tf_op | source)
XLA Modules:
  0.0 64.7 jit_solution(16555959046347952483)
XLA Ops:
  0.6 0.0 copy-start.2
  0.6 0.0 copy-start.4
  0.7 0.0 copy-start.9
  0.7 0.0 copy-start.5
  0.7 0.0 copy-start
  0.7 0.0 copy-start.7
  0.7 0.0 copy-start.6
  0.7 0.0 copy-start.3
  0.7 0.0 copy-start.8
  0.7 0.0 copy-start.1
  0.7 3.8 %copy.17 = bf16[2,1,64,12,512]{4,3,2,0,1:T(8,128)(2,1)} copy(bf16[2,1,64,12,512]{4,2,3,1,0:T(8,128)(2,1)} %param.19) | data formatting | bytes 3145728 | tf_op args[8]
  4.5 0.0 copy-done.2
  4.5 0.0 copy-done.4
  4.5 0.0 copy-done.9
  4.6 0.0 copy-done.5
  4.6 0.0 copy-done
  4.6 0.0 copy-done.7
  4.6 0.0 copy-done.6
  4.6 0.0 copy-done.3
  4.6 0.0 copy-done.8
  4.6 0.0 copy-done.1
  4.6 56.9 %patch_window_kernel.1 = (bf16[2,64,12,512]{3,2,1,0:T(8,128)(2,1)S(1)}, f32[16,20]{1,0:T(8,128)S(1)}, f32[16,128]{1,0:T(8,128)S(1)}) custom-call(bf16[2,320,768]{2,1,0:T(8,128)(2,1)S(1)} %bitcast.9, s32[5]{0:T(128)S(1)} %copy-done.8, bf16[3,16,512]{2,1,0:T(8,128)(2,1)S(1)} %copy-done.3, bf16[16,20]{1,0:T(8,128)(2,1)S(1)} %bitcast.11, ...), custom_call_target="tpu_custom_call" | custom-call | tf_op jit(solution)/shard_map/patch_window_kernel/pallas_call | solution.py:302
  61.5 2.0 %copy.15 = bf16[2,1,64,12,512]{4,2,3,1,0:T(8,128)(2,1)} copy(bf16[2,1,64,12,512]{4,3,2,0,1:T(8,128)(2,1)S(1)} %bitcast.8) | data formatting | bytes 3145728
  63.5 0.6 copy.20
  64.1 0.6 copy.21
Async XLA Ops:
  0.6 3.9 %copy-start.2 = (f32[192,192]{1,0:T(8,128)S(1)}, f32[192,192]{1,0:T(8,128)}, u32[]{:S(2)}) copy-start(f32[192,192]{1,0:T(8,128)} %constant.5.clone.same) | copy-start | bytes 442372
  0.6 3.9 %copy-start.4 = (bf16[192,96]{1,0:T(8,128)(2,1)S(1)}, bf16[192,96]{1,0:T(8,128)(2,1)}, u32[]{:S(2)}) copy-start(bf16[192,96]{1,0:T(8,128)(2,1)} %constant.4.clone.pick) | copy-start | bytes 110596
  0.7 3.9 %copy-start.9 = (s32[64]{0:T(128)S(1)}, s32[64]{0:T(128)}, u32[]{:S(2)}) copy-start(s32[64]{0:T(128)} %param.18) | copy-start | bytes 772
  0.7 3.9 %copy-start.5 = (bf16[96,96]{1,0:T(8,128)(2,1)S(1)}, bf16[96,96]{1,0:T(8,128)(2,1)}, u32[]{:S(2)}) copy-start(bf16[96,96]{1,0:T(8,128)(2,1)} %mixer.1) | copy-start | bytes 55300
  0.7 3.9 %copy-start = (bf16[4,512,512]{2,1,0:T(8,128)(2,1)S(1)}, bf16[4,512,512]{2,1,0:T(8,128)(2,1)}, u32[]{:S(2)}) copy-start(bf16[4,512,512]{2,1,0:T(8,128)(2,1)} %level_w.1) | copy-start | bytes 6291460
  0.7 3.9 %copy-start.7 = (bf16[16,128]{1,0:T(8,128)(2,1)S(1)}, bf16[16,128]{1,0:T(8,128)(2,1)}, u32[]{:S(2)}) copy-start(bf16[16,128]{1,0:T(8,128)(2,1)} %up.1) | copy-start | bytes 12292
  0.7 3.9 %copy-start.6 = (bf16[20,16]{0,1:T(8,128)(2,1)S(1)}, bf16[20,16]{0,1:T(8,128)(2,1)}, u32[]{:S(2)}) copy-start(bf16[20,16]{0,1:T(8,128)(2,1)} %param.14) | copy-start | bytes 1924
  0.7 3.9 %copy-start.3 = (bf16[3,16,512]{2,1,0:T(8,128)(2,1)S(1)}, bf16[3,16,512]{2,1,0:T(8,128)(2,1)}, u32[]{:S(2)}) copy-start(bf16[3,16,512]{2,1,0:T(8,128)(2,1)} %frozen.1) | copy-start | bytes 147460
  0.7 3.9 %copy-start.8 = (s32[5]{0:T(128)S(1)}, s32[5]{0:T(128)}, u32[]{:S(2)}) copy-start(s32[5]{0:T(128)} %vgi.1) | copy-start | bytes 64
  0.7 3.9 %copy-start.1 = (bf16[2,4,80,1,768]{4,2,3,1,0:T(8,128)(2,1)S(1)}, bf16[2,4,80,1,768]{4,2,3,1,0:T(8,128)(2,1)}, u32[]{:S(2)}) copy-start(bf16[2,4,80,1,768]{4,2,3,1,0:T(8,128)(2,1)} %param.11) | copy-start | bytes 2949124
